TPU v7x, 256 devices: a whole 4x4x8 slice. The times are simulated.
256 devices in a mesh: grp: 128 (over z, x, y), rep: 2 (over core).
Axes of the slice: x: 4, y: 4, z: 8, core: 2. Of those that a mesh axis runs over, the one named last changes fastest.
Arguments:
- snapshots: float32 [128, 2048, 1024], P('grp', 'rep'), may hold values from -6 to 6
- row_factor: float32 [2048, 128], P('rep'), may hold values from -0.125 to 0.125
- time_factor: float32 [128, 64], replicated, may hold values from -0.5 to 0.5
Outputs:
- new_rows: float32 [2048, 128], P('rep')
- new_time: float32 [128, 64], replicated
All inputs are finite; a program needn't handle non-finite values.
Results may differ from a plain program's by a relative error of at most 0.0001.
Values sent between devices are 32-bit elements; how exact they have to be, the bound alone decides.
A program may use at most 64 MiB of HBM per device.

v0:
```python
import math
import jax
import jax.numpy as jnp
from jax import lax
from jax.sharding import PartitionSpec as P

ROWS = 2048
STEPS = 8


def highdot(left, right):
    return jnp.dot(left, right, precision=lax.Precision.HIGHEST, preferred_element_type=jnp.float32)


def orthogonalize(start_matrix):
    total = jnp.sum(start_matrix * start_matrix)
    iterate = start_matrix / jnp.sqrt(total + 1e-06)
    for step_index in range(STEPS):
        inner = highdot(iterate.T, iterate)
        iterate = 1.5 * iterate - 0.5 * highdot(iterate, inner)
    return iterate


def on_device(snapshots, row_factor, time_factor):
    row_half = snapshots.shape[1]
    rank_row = row_factor.shape[1]
    projected = jnp.einsum("tij,ia->tja", snapshots, row_factor, precision=lax.Precision.HIGHEST)
    summed = lax.psum(projected, "rep")
    owned = lax.all_to_all(summed, "grp", split_axis=1, concat_axis=0, tiled=True)
    snaps = owned.shape[0]
    width = owned.shape[1] * rank_row
    flat = owned.reshape(snaps, width)
    halfwidth = width // 2
    portion = lax.dynamic_slice_in_dim(flat, lax.axis_index("rep") * halfwidth, halfwidth, 1)
    gram_part = highdot(portion, portion.T)
    gram_total = lax.psum(gram_part, ("grp", "rep"))
    start_time = highdot(gram_total, time_factor)
    basis_time = orthogonalize(start_time)
    mixer = highdot(basis_time, basis_time.T)
    weights = highdot(mixer, flat).reshape(owned.shape)
    returned = lax.all_to_all(weights, "grp", split_axis=0, concat_axis=1, tiled=True)
    own_rows = lax.psum_scatter(
        jnp.einsum("tij,tja->ia", snapshots, returned, precision=lax.Precision.HIGHEST),
        "grp",
        scatter_dimension=0,
        tiled=True,
    )
    half_block = lax.all_gather(own_rows, "grp", axis=0, tiled=True)
    all_block = lax.all_gather(half_block, "rep", axis=0, tiled=True)
    basis = orthogonalize(all_block)
    new_rows = lax.dynamic_slice_in_dim(basis, lax.axis_index("rep") * row_half, row_half, 0)
    return (new_rows * math.sqrt(ROWS), basis_time * math.sqrt(snaps))


def solution(mesh):
    return jax.shard_map(
        on_device,
        mesh=mesh,
        in_specs=(P("grp", "rep", None), P("rep", None), P()),
        out_specs=(P("rep", None), P()),
        check_vma=False,
    )
```

profile of v0, /device:TPU:1, one launch (start us, length us, event | category | flops | bytes accessed | tf_op | source)
XLA Modules:
  0.0 982.5 jit_solution(4008514134810224522)
XLA Ops:
  7.2 1.0 copy-done
  8.2 9.6 fusion.11
  17.9 34.2 %all-reduce.5.cloned.1.call-done = f32[1,1024,128]{2,1,0:T(8,128)} async-done(((f32[1,1024,128]{2,1,0:T(8,128)}), f32[1,1024,128]{2,1,0:T(8,128)}) %all-reduce.5.cloned.1.call-update) | async-done | bytes 524304 | tf_op jit(solution)/shard_map/psum | solution.py:28
  52.1 13.6 %all-to-all-start = ((f32[1,1024,128]{2,0,1:T(1,128)}), f32[1,1024,128]{2,0,1:T(1,128)S(1)}, u32[]{:S(2)}, u32[]{:S(2)}) async-start(f32[1,1024,128]{2,0,1:T(1,128)} %bitcast.92), calls=%async_computation | async-start | bytes 1048576 | tf_op jit(solution)/shard_map/all_to_all | solution.py:29
  65.7 19.0 %all-to-all-done = f32[1,1024,128]{2,0,1:T(1,128)S(1)} async-done(((f32[1,1024,128]{2,0,1:T(1,128)}), f32[1,1024,128]{2,0,1:T(1,128)S(1)}, u32[]{:S(2)}, u32[]{:S(2)}) %all-to-all-start) | async-done | bytes 524320 | tf_op jit(solution)/shard_map/all_to_all | solution.py:29
  84.6 0.5 broadcast.53
  85.2 1.9 reduce.3
  87.1 1.0 fusion.29
  88.2 0.5 all-reduce.9.cloned.1.call-start
  88.7 0.2 copy.27
  88.9 231.8 %all-reduce.7.cloned.1.call-done = f32[128,128]{1,0:T(8,128)} async-done(((f32[128,128]{1,0:T(8,128)}), f32[128,128]{1,0:T(8,128)}) %all-reduce.7.cloned.1.call-update) | async-done | bytes 65552 | tf_op jit(solution)/shard_map/psum | solution.py:36
  320.7 1.7 multiply_reduce_fusion.1
  323.3 0.2 fusion.24
  323.8 0.2 fusion.23
  324.2 0.2 fusion.22
  324.6 0.2 fusion.21
  325.1 0.2 fusion.20
  325.5 0.2 fusion.19
  325.9 0.2 fusion.18
  326.4 0.9 broadcast_multiply_fusion
  327.2 0.3 convolution_bitcast_fusion
  327.5 0.6 fusion.40
  328.1 0.3 copy.28
  328.4 25.9 %all_to_all.8 = f32[128,8,128]{2,1,0:T(8,128)S(1)} all-to-all(f32[128,8,128]{2,1,0:T(8,128)S(1)} %copy.28), channel_id=1, replica_groups=mesh['grp'=128,'rep'=2] {'grp'}, dimensions={0} | all-to-all | bytes 1048576 | tf_op jit(solution)/shard_map/all_to_all | solution.py:41
  354.3 5.4 fusion.14
  359.8 0.6 dynamic-slice
  360.9 206.4 %all-reduce.9.cloned.1.call-done = f32[1024,128]{0,1:T(8,128)} async-done(((f32[1024,128]{0,1:T(8,128)}), f32[1024,128]{0,1:T(8,128)}) %all-reduce.9.cloned.1.call-update) | async-done | bytes 524304
  567.4 0.9 constant_dynamic-slice_fusion
  568.3 309.8 %all_gather.6 = f32[1024,128]{1,0:T(8,128)} all-gather(f32[8,128]{1,0:T(8,128)S(1)} %copy.29), channel_id=1, replica_groups=mesh['grp'=128,'rep'=2] {'grp'}, dimensions={0}, use_global_device_ids=true | all-gather | bytes 528384 | tf_op jit(solution)/shard_map/all_gather | solution.py:48
  878.2 69.5 %all-gather.2.cloned.1.call-done = f32[2048,128]{1,0:T(8,128)} async-done(((f32[1024,128]{1,0:T(8,128)}), f32[2048,128]{1,0:T(8,128)}) %all-gather.2.cloned.1.call-update) | async-done | bytes 1048592 | tf_op jit(solution)/shard_map/all_gather | solution.py:49
  947.7 2.2 multiply_reduce_fusion
  950.6 3.4 fusion.28
  954.0 1.0 fusion.10
  955.0 1.8 fusion.41
  956.8 1.0 fusion.9
  957.8 1.8 fusion.42
  959.6 1.0 fusion.8
  960.6 1.8 fusion.43
  962.4 1.2 fusion.7
  963.6 1.8 fusion.44
  965.4 1.0 fusion.6
  966.4 1.8 fusion.45
  968.2 1.0 fusion.5
  969.2 1.8 fusion.46
  971.0 1.0 fusion.4
  972.0 1.8 fusion.47
  973.9 1.0 fusion.48
  974.8 0.9 fusion.26
  (26 shorter events, 1.8 us)
Async XLA Ops:
  7.2 1.0 copy-start
  7.2 313.5 %copy-start.3 = (f32[128,64]{0,1:T(8,128)S(1)}, f32[128,64]{0,1:T(8,128)}, u32[]{:S(2)}) copy-start(f32[128,64]{0,1:T(8,128)} %param.5) | copy-start | bytes 98308
  7.2 44.9 %all-reduce.5.cloned.1.call-start = ((), (), s32[]{:S(2)}) async-start(), calls=%async_computation.2 | async-start | bytes 1048576 | tf_op jit(solution)/shard_map/psum | solution.py:28
  52.1 32.6 %all-to-all-start = ((f32[1,1024,128]{2,0,1:T(1,128)}), f32[1,1024,128]{2,0,1:T(1,128)S(1)}, u32[]{:S(2)}, u32[]{:S(2)}) async-start(f32[1,1024,128]{2,0,1:T(1,128)} %bitcast.92), calls=%async_computation | async-start | bytes 1048576 | tf_op jit(solution)/shard_map/all_to_all | solution.py:29
  65.6 255.1 %all-reduce.7.cloned.1.call-start = ((), (), s32[]{:S(2)}) async-start(), calls=%async_computation.3 | async-start | bytes 131072 | tf_op jit(solution)/shard_map/psum | solution.py:36
  88.2 479.2 %all-reduce.9.cloned.1.call-start = ((), (), s32[]{:S(2)}) async-start(), calls=%async_computation.5 | async-start | bytes 1048576
  323.1 31.2 %copy-start.1 = (f32[1,1024,1024]{2,1,0:T(8,128)S(1)}, f32[1,1024,1024]{2,1,0:T(8,128)}, u32[]{:S(2)}) copy-start(f32[1,1024,1024]{2,1,0:T(8,128)} %param.3) | copy-start | bytes 12582916
  328.1 31.7 %copy-start.4 = (u32[256]{0:T(256)S(1)}, u32[256]{0:T(256)}, u32[]{:S(2)}) copy-start(u32[256]{0:T(256)} %constant.29) | copy-start | bytes 3076
  359.7 588.0 %all-gather.2.cloned.1.call-start = ((), (), s32[]{:S(2)}) async-start(), calls=%async_computation.4 | async-start | bytes 1572864 | tf_op jit(solution)/shard_map/all_gather | solution.py:49
  947.7 6.3 copy-start.2
Sparse Core Ops, SparseCore 0:
  18.0 34.0 all-reduce.4
  88.3 232.3 all-reduce.6
  359.8 207.4 all-reduce.8
  878.3 69.3 all-gather.1
where the time goes:
time: 990 us; the launch traced here: 982 us
  waiting for transfers between devices  561 us (57%)
  blocking collectives  336 us (34%)
  matrix products  46.7 us (5%)
  between operations  16.3 us (2%)
  starting transfers between devices  14.2 us (1%)
    all_gather x1, blocking collectives, on_device(): half_block = lax.all_gather(own_rows, 'grp', axis=0, tiled=True)  310 us
    psum x1, waiting for transfers between devices, on_device(): gram_total = lax.psum(gram_part, ('grp', 'rep'))  232 us
    unnamed x5, waiting for transfers between devices  206 us
    all_gather x1, waiting for transfers between devices, on_device(): all_block = lax.all_gather(half_block, 'rep', axis=0, tiled=True)  69.5 us
    psum x1, waiting for transfers between devices, on_device(): summed = lax.psum(projected, 'rep')  34.2 us
    dot_general x36, matrix products, highdot(): jnp.dot(left, right, precision=lax.Precision.HIGHEST, preferred_element_t...  31.7 us
    all_to_all x1, blocking collectives, on_device(): lax.all_to_all(weights, 'grp', split_axis=0, concat_axis=1, tiled=True)  25.9 us
  transfers between devices with their start and end apart: 5, of which 5 were waited for; matrix products, arithmetic and copies ran while one was open for 0% of the time, Pallas kernels for 0%

commit v1 on v0

--- a/solution.py
+++ b/solution.py
@@ -33,7 +33,7 @@
     halfwidth = width // 2
     portion = lax.dynamic_slice_in_dim(flat, lax.axis_index("rep") * halfwidth, halfwidth, 1)
     gram_part = highdot(portion, portion.T)
-    gram_total = lax.psum(gram_part, ("grp", "rep"))
+    gram_total = jnp.sum(lax.all_gather(gram_part, ("grp", "rep")), axis=0)
     start_time = highdot(gram_total, time_factor)
     basis_time = orthogonalize(start_time)
     mixer = highdot(basis_time, basis_time.T)

time: 990 us -> 885 us (0.89)
  waiting for transfers between devices: 561 us -> 447 us
    psum x1 -> x0, waiting for transfers between devices: 232 us -> none  [on_device(): gram_total = lax.psum(gram_part, ('grp', 'rep'))]
    all_gather x0 -> x1, waiting for transfers between devices: none -> 119 us  [on_device(): gram_total = jnp.sum(lax.all_gather(gram_part, ('grp', 'rep')), axis=0)]
where the time goes in v1:
time: 885 us; the launch traced here: 877 us
  waiting for transfers between devices  447 us (51%)
  blocking collectives  338 us (38%)
  matrix products  45.9 us (5%)
  between operations  16.3 us (2%)
  starting transfers between devices  14.2 us (2%)
  other arithmetic  11.6 us (1%)
    all_gather x1, blocking collectives, on_device(): half_block = lax.all_gather(own_rows, 'grp', axis=0, tiled=True)  310 us
    unnamed x5, waiting for transfers between devices  205 us
    all_gather x1, waiting for transfers between devices, on_device(): gram_total = jnp.sum(lax.all_gather(gram_part, ('grp', 'rep')), axis=0)  119 us
    all_gather x1, waiting for transfers between devices, on_device(): all_block = lax.all_gather(half_block, 'rep', axis=0, tiled=True)  69.5 us
    psum x1, waiting for transfers between devices, on_device(): summed = lax.psum(projected, 'rep')  34.2 us
    dot_general x36, matrix products, highdot(): jnp.dot(left, right, precision=lax.Precision.HIGHEST, preferred_element_t...  30.9 us
    all_to_all x1, blocking collectives, on_device(): lax.all_to_all(weights, 'grp', split_axis=0, concat_axis=1, tiled=True)  28.5 us
    all_to_all x1, waiting for transfers between devices, on_device(): lax.all_to_all(summed, 'grp', split_axis=1, concat_axis=0, tiled=True)  19 us
  transfers between devices with their start and end apart: 5, of which 5 were waited for; matrix products, arithmetic and copies ran while one was open for 0% of the time, Pallas kernels for 0%

profile of v1, /device:TPU:1, one launch (start us, length us, event | category | flops | bytes accessed | tf_op | source)
XLA Modules:
  0.0 877.1 jit_solution(12701275597162375894)
XLA Ops:
  7.2 1.0 copy-done
  8.2 9.6 %fusion.11 = f32[1,1024,128]{2,1,0:T(8,128)} fusion(f32[1024,128]{1,0:T(8,128)S(1)} %copy-done, f32[1,1024,1024]{2,1,0:T(8,128)} %param.3), kind=kOutput, calls=%fused_computation.18 | convolution fusion | flops 1610612736 | bytes 5242880 | tf_op jit(solution)/shard_map/tij,ia->tja/dot_general | solution.py:27
  17.9 34.2 %all-reduce.4.cloned.1.call-done = f32[1,1024,128]{2,1,0:T(8,128)} async-done(((f32[1,1024,128]{2,1,0:T(8,128)}), f32[1,1024,128]{2,1,0:T(8,128)}) %all-reduce.4.cloned.1.call-update) | async-done | bytes 524304 | tf_op jit(solution)/shard_map/psum | solution.py:28
  52.1 13.6 %all-to-all-start = ((f32[1,1024,128]{2,0,1:T(1,128)}), f32[1,1024,128]{2,0,1:T(1,128)S(1)}, u32[]{:S(2)}, u32[]{:S(2)}) async-start(f32[1,1024,128]{2,0,1:T(1,128)} %bitcast.94), calls=%async_computation | async-start | bytes 1048576 | tf_op jit(solution)/shard_map/all_to_all | solution.py:29
  65.7 19.0 %all-to-all-done = f32[1,1024,128]{2,0,1:T(1,128)S(1)} async-done(((f32[1,1024,128]{2,0,1:T(1,128)}), f32[1,1024,128]{2,0,1:T(1,128)S(1)}, u32[]{:S(2)}, u32[]{:S(2)}) %all-to-all-start) | async-done | bytes 524320 | tf_op jit(solution)/shard_map/all_to_all | solution.py:29
  84.6 0.5 broadcast.53
  85.2 1.9 reduce.3
  87.1 1.0 fusion.29
  88.2 0.5 all-reduce.6.cloned.1.call-start
  88.9 119.2 %all-gather.6.cloned.1.call-done = f32[32768,128]{1,0:T(8,128)} async-done(((f32[128,128]{1,0:T(8,128)}), f32[32768,128]{1,0:T(8,128)}) %all-gather.6.cloned.1.call-update) | async-done | bytes 16777232 | tf_op jit(solution)/shard_map/all_gather | solution.py:36
  208.1 6.6 reduce_sum.27
  214.7 0.8 multiply_reduce_fusion.1
  216.5 0.2 fusion.24
  216.9 0.2 fusion.23
  217.4 0.2 fusion.22
  217.8 0.2 fusion.21
  218.2 0.2 fusion.20
  218.7 0.2 fusion.19
  219.1 0.2 fusion.18
  219.5 0.9 broadcast_multiply_fusion
  220.4 0.3 convolution_bitcast_fusion
  220.7 0.6 fusion.40
  221.3 0.3 copy.28
  221.6 28.5 %all_to_all.8 = f32[128,8,128]{2,1,0:T(8,128)S(1)} all-to-all(f32[128,8,128]{2,1,0:T(8,128)S(1)} %copy.28), channel_id=1, replica_groups=mesh['grp'=128,'rep'=2] {'grp'}, dimensions={0} | all-to-all | bytes 1048576 | tf_op jit(solution)/shard_map/all_to_all | solution.py:41
  250.2 5.4 fusion.14
  255.6 0.6 dynamic-slice
  256.7 205.2 %all-reduce.6.cloned.1.call-done = f32[1024,128]{0,1:T(8,128)} async-done(((f32[1024,128]{0,1:T(8,128)}), f32[1024,128]{0,1:T(8,128)}) %all-reduce.6.cloned.1.call-update) | async-done | bytes 524304
  462.0 0.9 constant_dynamic-slice_fusion
  462.9 309.8 %all_gather.14 = f32[1024,128]{1,0:T(8,128)} all-gather(f32[8,128]{1,0:T(8,128)S(1)} %copy.29), channel_id=1, replica_groups=mesh['grp'=128,'rep'=2] {'grp'}, dimensions={0}, use_global_device_ids=true | all-gather | bytes 528384 | tf_op jit(solution)/shard_map/all_gather | solution.py:48
  772.8 69.5 %all-gather.4.cloned.1.call-done = f32[2048,128]{1,0:T(8,128)} async-done(((f32[1024,128]{1,0:T(8,128)}), f32[2048,128]{1,0:T(8,128)}) %all-gather.4.cloned.1.call-update) | async-done | bytes 1048592 | tf_op jit(solution)/shard_map/all_gather | solution.py:49
  842.3 2.2 multiply_reduce_fusion
  845.2 3.4 fusion.28
  848.6 1.0 fusion.10
  849.6 1.8 fusion.41
  851.4 1.0 fusion.9
  852.4 1.8 fusion.42
  854.2 1.0 fusion.8
  855.2 1.8 fusion.43
  857.0 1.2 fusion.7
  858.2 1.8 fusion.44
  860.1 1.0 fusion.6
  861.0 1.8 fusion.45
  862.9 1.0 fusion.5
  863.8 1.8 fusion.46
  865.7 1.0 fusion.4
  866.6 1.8 fusion.47
  868.5 1.0 fusion.48
  869.4 0.9 fusion.26
  (27 shorter events, 2.0 us)
Async XLA Ops:
  7.2 1.0 copy-start
  7.2 44.9 %all-reduce.4.cloned.1.call-start = ((), (), s32[]{:S(2)}) async-start(), calls=%async_computation.2 | async-start | bytes 1048576 | tf_op jit(solution)/shard_map/psum | solution.py:28
  52.1 32.6 %all-to-all-start = ((f32[1,1024,128]{2,0,1:T(1,128)}), f32[1,1024,128]{2,0,1:T(1,128)S(1)}, u32[]{:S(2)}, u32[]{:S(2)}) async-start(f32[1,1024,128]{2,0,1:T(1,128)} %bitcast.94), calls=%async_computation | async-start | bytes 1048576 | tf_op jit(solution)/shard_map/all_to_all | solution.py:29
  65.6 142.5 %all-gather.6.cloned.1.call-start = ((), (), s32[]{:S(2)}) async-start(), calls=%async_computation.4 | async-start | bytes 16842752 | tf_op jit(solution)/shard_map/all_gather | solution.py:36
  88.2 373.8 %all-reduce.6.cloned.1.call-start = ((), (), s32[]{:S(2)}) async-start(), calls=%async_computation.5 | async-start | bytes 1048576
  208.1 6.6 copy-start.3
  216.3 33.9 %copy-start.1 = (f32[1,1024,1024]{2,1,0:T(8,128)S(1)}, f32[1,1024,1024]{2,1,0:T(8,128)}, u32[]{:S(2)}) copy-start(f32[1,1024,1024]{2,1,0:T(8,128)} %param.3) | copy-start | bytes 12582916
  221.3 34.3 %copy-start.4 = (u32[256]{0:T(256)S(1)}, u32[256]{0:T(256)}, u32[]{:S(2)}) copy-start(u32[256]{0:T(256)} %constant.29) | copy-start | bytes 3076
  255.5 586.8 %all-gather.4.cloned.1.call-start = ((), (), s32[]{:S(2)}) async-start(), calls=%async_computation.3 | async-start | bytes 1572864 | tf_op jit(solution)/shard_map/all_gather | solution.py:49
  842.3 6.3 copy-start.2
Sparse Core Ops, SparseCore 0:
  18.0 34.0 all-reduce.3
  88.3 119.7 all-gather.5
  255.7 206.2 all-reduce.5
  772.9 69.3 all-gather.3
